TPU v7x, 256 devices: a whole 4x4x8 slice. The times are simulated.
256 devices in a mesh: rep: 8 (over z), fsdp: 32 (over y, x, core).
Axes of the slice: x: 4, y: 4, z: 8, core: 2. Of those that a mesh axis runs over, the one named last changes fastest.
Arguments:
- tokens: bfloat16 [65536, 4096], P(('rep', 'fsdp')), may hold values from -6 to 6
- out_grad: bfloat16 [65536, 14336], P(('rep', 'fsdp')), may hold values from -6 to 6
- weight_blocks: bfloat16 [256, 128, 128], P('fsdp'), may hold values from -0.1875 to 0.1875
- block_row: int32 [256], replicated, may hold values from 0 to 31, as said below
- block_col: int32 [256], replicated, may hold values from 0 to 111
- send_list: int32 [32, 8, 3], P('fsdp'), may hold values from 0 to 8, as said below
Outputs:
- token_grad: bfloat16 [65536, 4096], P(('rep', 'fsdp'))
- grad_owned: float32 [8, 32, 3, 128, 128], P('rep', 'fsdp')
Inputs may be any that keep to these rules, and one draw needn't show every extreme that they name: The pairs (block_row[k], block_col[k]) are all distinct. For each f, every local block number 0 to 7 stands exactly once in send_list[f] over all owners and slots, in increasing order within an owner's slots, followed by the pad value 8; for each f some owner fills all 3 slots.
All inputs are finite; a program needn't handle non-finite values.
Results may differ from a plain program's by a relative error of at most 0.001.
Values may be sent and summed in bfloat16 or wider, within the bound.
No kernel may reach another device: no remote copies, remote signals or barrier semaphores. Data moves between devices by JAX's collectives and lax.ppermute only.
A program may use at most 256 MiB of HBM per device.

v0:
```python
import jax
import jax.numpy as jnp
from jax import lax
from jax.sharding import PartitionSpec as P


def spread(products, row_ids, row_count):
    chosen = (row_ids[:, None] == jnp.arange(row_count, dtype=jnp.int32)[None, :]).astype(
        jnp.float32
    )
    return jnp.einsum("tnk,nq->tqk", products, chosen, precision=lax.Precision.HIGHEST)


def block_products(grad_cols, row_ids, col_ids, pieces, row_count):
    picked = jnp.take(grad_cols, col_ids, axis=1)
    products = jnp.einsum("tnc,nrc->tnr", picked, pieces, preferred_element_type=jnp.float32)
    return spread(products, row_ids, row_count)


def block_sums(features, grad_cols, row_ids, col_ids):
    left_cols = jnp.take(features, row_ids, axis=1)
    right_cols = jnp.take(grad_cols, col_ids, axis=1)
    return jnp.einsum("tnr,tnc->nrc", left_cols, right_cols, preferred_element_type=jnp.float32)


def local(tokens, out_grad, weight_blocks, block_row, block_col, send_list):
    rows_here = tokens.shape[0]
    block_size = weight_blocks.shape[1]
    row_count = tokens.shape[1] // block_size
    col_count = out_grad.shape[1] // block_size
    features = tokens.reshape(rows_here, row_count, block_size)
    grad_cols = out_grad.reshape(rows_here, col_count, block_size)
    all_blocks = lax.all_gather(weight_blocks, "fsdp", axis=0, tiled=True)
    spread_sum = block_products(grad_cols, block_row, block_col, all_blocks, row_count)
    token_grad = spread_sum.reshape(rows_here, row_count * block_size).astype(jnp.bfloat16)
    rep_count = lax.axis_size("rep")
    fsdp_count = lax.axis_size("fsdp")
    grad_scale = float(rows_here * rep_count * fsdp_count) ** (-0.5)
    empty_block = jnp.zeros((1, block_size, block_size), jnp.float32)
    peer_lists = send_list[0]
    shard_sums = lax.psum_scatter(
        block_sums(features, grad_cols, block_row, block_col),
        "fsdp",
        scatter_dimension=0,
        tiled=True,
    )
    padded = jnp.concatenate([shard_sums, empty_block], axis=0)
    outgoing = jnp.take(padded, peer_lists, axis=0)
    owned_blocks = jnp.sum(
        lax.all_to_all(outgoing, "rep", split_axis=0, concat_axis=0, tiled=True), axis=0
    )
    grad_owned = (owned_blocks * grad_scale)[None, None]
    return (token_grad, grad_owned)


def solution(mesh):
    return jax.shard_map(
        local,
        mesh=mesh,
        in_specs=(
            P(("rep", "fsdp"), None),
            P(("rep", "fsdp"), None),
            P("fsdp", None, None),
            P(),
            P(),
            P("fsdp", None, None),
        ),
        out_specs=(P(("rep", "fsdp"), None), P("rep", "fsdp", None, None, None)),
        check_vma=False,
    )
```

profile of v0, /device:TPU:1, one launch (start us, length us, event | category | flops | bytes accessed | tf_op | source)
XLA Modules:
  0.0 343.0 jit_solution(7877266867744375647)
XLA Ops:
  7.2 0.0 copy-start
  7.2 0.0 reduce-scatter.2.cloned.1.call-start
  7.2 0.8 compare_select_fusion.2
  8.0 0.7 compare_and_fusion
  8.7 0.7 compare_select_fusion.3
  9.4 0.7 compare_and_fusion.1
  10.1 10.2 %copy.21 = bf16[256,14336]{0,1:T(8,128)(2,1)} copy(bf16[256,14336]{1,0:T(8,128)(2,1)} %param.9) | data formatting | bytes 14680064 | tf_op args[1]
  20.3 10.5 %copy.22 = bf16[256,112,128]{2,0,1:T(8,128)(2,1)} copy(bf16[256,112,128]{0,2,1:T(8,128)(2,1)} %bitcast.34) | data formatting | bytes 14680064 | tf_op jit(solution)/shard_map/reshape | solution.py:32
  30.8 0.0 copy-done
  30.8 2.5 copy.25
  33.2 3.2 copy.26
  36.5 12.9 %gather_fusion.2 = bf16[256,256,128]{2,1,0:T(8,128)(2,1)} fusion(bf16[256,112,128]{2,0,1:T(8,128)(2,1)} %copy.22, s32[1024]{0:T(1024)S(1)} %pad_clamp_fusion.2), kind=kCustom, calls=%fused_computation.clone | custom fusion | bytes 33555456 | tf_op jit(solution)/shard_map/jit(_take)/gather | solution.py:15
  49.3 9.8 %gather_fusion = bf16[256,256,128]{2,1,0:T(8,128)(2,1)} fusion(bf16[256,32,128]{2,0,1:T(8,128)(2,1)S(1)} %copy.26, s32[1024]{0:T(1024)S(1)} %pad_clamp_fusion.1), kind=kCustom, calls=%fused_computation.1 | custom fusion | bytes 33555456 | tf_op jit(solution)/shard_map/jit(_take)/gather | solution.py:21
  59.1 19.7 %fusion.2 = f32[256,128,128]{2,1,0:T(8,128)} fusion(bf16[256,256,128]{2,1,0:T(8,128)(2,1)} %gather_fusion, pred[256]{0:T(512)(128)(4,1)S(1)} %compare_and_fusion.1, bf16[256,256,128]{2,1,0:T(8,128)(2,1)} %gather_fusion.2, pred[256]{0:T(512)(128)(4,1)S(1)} %compare_and_fusion), kind=kOutput, calls=%fused_computation.5 | convolution fusion | flops 2164260864 | bytes 50332160 | tf_op jit(solution)/shard_map/tnr,tnc->nrc/dot_general | solution.py:23
  78.8 0.0 copy-start.1
  78.8 0.0 reduce-scatter.2.cloned.1.call-update
  78.8 0.0 all-gather.2.cloned.1.call-start
  78.9 0.7 all-gather.2.cloned.1.call-update
  79.6 0.0 copy-done.1
  79.6 0.1 copy.28
  79.7 0.1 reshape.86
  79.8 0.1 copy.24
  79.9 124.5 %reduce-scatter.2.cloned.1.call-done = f32[8,128,128]{2,1,0:T(8,128)} async-done(((f32[256,128,128]{2,1,0:T(8,128)}), f32[8,128,128]{2,1,0:T(8,128)}) %reduce-scatter.2.cloned.1.call-update) | async-done | bytes 524304 | tf_op jit(solution)/shard_map/reduce_scatter | solution.py:41
  204.4 1.1 concatenate.3
  205.5 0.6 gather_fusion.1
  206.1 1.3 broadcast_select_fusion.3
  207.4 6.7 %all-to-all-start = ((f32[8,3,128,128]{3,2,1,0:T(8,128)}), f32[8,3,128,128]{3,2,1,0:T(8,128)}, u32[]{:S(2)}, u32[]{:S(2)}) async-start(f32[8,3,128,128]{3,2,1,0:T(8,128)} %broadcast_select_fusion.3), calls=%async_computation.1 | async-start | bytes 3145728 | tf_op jit(solution)/shard_map/all_to_all | solution.py:50
  214.2 0.0 copy-start.2
  214.2 51.8 %all-gather.2.cloned.1.call-done = bf16[256,128,128]{2,1,0:T(8,128)(2,1)} async-done(((bf16[8,128,128]{2,1,0:T(8,128)(2,1)}), bf16[256,128,128]{2,1,0:T(8,128)(2,1)}) %all-gather.2.cloned.1.call-update) | async-done | bytes 8388624 | tf_op jit(solution)/shard_map/all_gather | solution.py:33
  266.0 20.1 %fusion.9 = f32[256,256,128]{2,0,1:T(8,128)} fusion(bf16[256,128,128]{2,1,0:T(8,128)(2,1)} %all-gather.2.cloned.1.call-done, bf16[256,256,128]{2,1,0:T(8,128)(2,1)} %gather_fusion.2, pred[256]{0:T(512)(128)(4,1)S(1)} %compare_and_fusion), kind=kOutput, calls=%fused_computation.13 | convolution fusion | flops 2155872256 | bytes 58720512 | tf_op jit(solution)/shard_map/tnc,nrc->tnr/dot_general | solution.py:16
  286.1 0.0 copy-done.2
  286.1 45.6 %fusion.13 = bf16[32,256,128]{2,0,1:T(8,128)(2,1)S(1)} fusion(f32[256,256,128]{2,0,1:T(8,128)} %fusion.9, s32[256]{0:T(256)S(1)} %copy-done.2), kind=kOutput, calls=%fused_computation.16 | convolution fusion | flops 3222282240 | bytes 35652608 | tf_op jit(solution)/shard_map/tnk,nq->tqk/dot_general | solution.py:11
  331.7 2.3 copy.40
  334.0 0.0 all-to-all-done
  334.0 1.5 reduce_sum.9
  335.5 0.7 multiply_bitcast_fusion
  (5 shorter events, 0.0 us)
Async XLA Ops:
  7.2 23.6 %copy-start = (bf16[256,4096]{1,0:T(8,128)(2,1)S(1)}, bf16[256,4096]{1,0:T(8,128)(2,1)}, u32[]{:S(2)}) copy-start(bf16[256,4096]{1,0:T(8,128)(2,1)} %param.8) | copy-start | bytes 6291460
  7.2 197.2 %reduce-scatter.2.cloned.1.call-start = ((), (), s32[]{:S(2)}) async-start(), calls=%async_computation.3 | async-start | bytes 17301504 | tf_op jit(solution)/shard_map/reduce_scatter | solution.py:41
  78.8 0.8 copy-start.1
  78.8 187.1 %all-gather.2.cloned.1.call-start = ((), (), s32[]{:S(2)}) async-start(), calls=%async_computation.2 | async-start | bytes 8650752 | tf_op jit(solution)/shard_map/all_gather | solution.py:33
  207.4 126.5 %all-to-all-start = ((f32[8,3,128,128]{3,2,1,0:T(8,128)}), f32[8,3,128,128]{3,2,1,0:T(8,128)}, u32[]{:S(2)}, u32[]{:S(2)}) async-start(f32[8,3,128,128]{3,2,1,0:T(8,128)} %broadcast_select_fusion.3), calls=%async_computation.1 | async-start | bytes 3145728 | tf_op jit(solution)/shard_map/all_to_all | solution.py:50
  214.2 71.9 %copy-start.2 = (s32[256]{0:T(256)S(1)}, s32[256]{0:T(256)}, u32[]{:S(2)}) copy-start(s32[256]{0:T(256)} %param.11) | copy-start | bytes 3076
Sparse Core Ops, SparseCore 0:
  79.0 125.3 reduce-scatter.1
  206.9 59.0 all-gather.1
where the time goes:
time: 344 us; the launch traced here: 343 us
  waiting for transfers between devices  177 us (51%)
  matrix products  85.4 us (25%)
  local copies, waits for them, and re-layouts  53.3 us (15%)
  between operations  14.1 us (4%)
  starting transfers between devices  6.82 us (2%)
  other arithmetic  6.41 us (2%)
    reduce_scatter x1, waiting for transfers between devices, local(): lax.psum_scatter(block_sums(features, grad_cols, block_row, block_col), '...  124 us
    all_gather x1, waiting for transfers between devices, local(): all_blocks = lax.all_gather(weight_blocks, 'fsdp', axis=0, tiled=True)  51.8 us
    dot_general x1, matrix products, spread(): jnp.einsum('tnk,nq->tqk', products, chosen, precision=lax.Precision.HIGHEST)  45.6 us
    dot_general x1, matrix products, block_products(): jnp.einsum('tnc,nrc->tnr', picked, pieces, preferred_element_type=jnp.flo...  20.1 us
    dot_general x1, matrix products, block_sums(): jnp.einsum('tnr,tnc->nrc', left_cols, right_cols, preferred_element_type=...  19.7 us
    unnamed x9, local copies, waits for them, and re-layouts  14.9 us
    gather x1, local copies, waits for them, and re-layouts, block_products(): picked = jnp.take(grad_cols, col_ids, axis=1)  12.9 us
    reshape x1, local copies, waits for them, and re-layouts, local(): grad_cols = out_grad.reshape(rows_here, col_count, block_size)  10.5 us
  transfers between devices with their start and end apart: 3, of which 2 were waited for; matrix products, arithmetic and copies ran while one was open for 21% of the time, Pallas kernels for 0%

commit v1 on v0

v1 whole, which is shorter than its diff:
```python
import functools

import jax
import jax.numpy as jnp
from jax import lax
from jax.experimental import pallas as pl
from jax.experimental.pallas import tpu as pltpu
from jax.sharding import PartitionSpec as P


SIDE = 4
CORES = 2
BS = 128
SIDEBAND = 16
PAIR = 2 * BS + SIDEBAND
UNITS = 16
UNROLL = 2
TOP = 8192.0
TINY = 1e-33
VMEM = pl.BlockSpec(memory_space=pltpu.VMEM)
SMEM = pl.BlockSpec(memory_space=pltpu.SMEM)


def fast(a):
    return pltpu.with_memory_space_constraint(a, pltpu.VMEM)


def encode(blocks, ref, base):
    grouped = [b.reshape(BS // SIDEBAND, SIDEBAND, BS) for b in blocks]
    largest = functools.reduce(jnp.maximum, [jnp.max(jnp.abs(g), axis=0) for g in grouped])
    side = largest.astype(jnp.bfloat16)
    top = side.astype(jnp.float32)
    scale = jnp.where(top > TINY, TOP / jnp.maximum(top, TINY), 0.0)
    for i, g in enumerate(grouped):
        u = g * scale[None]
        u2 = u * u
        u4 = u2 * u2
        y = (u4 * u4) * u
        ref[pl.ds(base + i * BS, BS), :] = y.reshape(BS, BS).astype(jnp.bfloat16)
    ref[pl.ds(base + len(blocks) * BS, SIDEBAND), :] = side


def decode(ref, base, count):
    side = ref[pl.ds(base + count * BS, SIDEBAND), :].astype(jnp.float32) * (1.0 / TOP)
    out = []
    for i in range(count):
        y = ref[pl.ds(base + i * BS, BS), :].astype(jnp.float32)
        r = jnp.exp2(jnp.log2(jnp.abs(y)) * (1.0 / 9.0))
        r = jnp.where(y < 0, -r, r).reshape(BS // SIDEBAND, SIDEBAND, BS)
        out.append((r * side[None]).reshape(BS, BS))
    return out


def place(me):
    core = lax.rem(me, CORES)
    chip = lax.div(me, CORES)
    return lax.div(chip, SIDE), lax.rem(chip, SIDE), core


def block_of(half, y, x, step, u):
    other = lax.div(u, 4)
    yy = jnp.where(half == 0, lax.rem(y + step, SIDE), other)
    xx = jnp.where(half == 0, other, lax.rem(x + step, SIDE))
    core = lax.rem(lax.div(u, 2), 2)
    return ((yy * SIDE + xx) * CORES + core) * 8 + half * 4 + lax.rem(u, 2) * 2


def product(tok, grad, row, col, k):
    left = tok[pl.ds(pl.multiple_of(row[k] * BS, BS), BS), :]
    right = grad[:, pl.ds(pl.multiple_of(col[k] * BS, BS), BS)]
    return jnp.dot(left, right, preferred_element_type=jnp.float32)


def first_kernel(steps, row, col, where, tok, grad, out):
    y, x, core = place(where[0])
    for n, step in enumerate(steps):

        def body(u, _, n=n, step=step):
            k = block_of(1 - core, y, x, step, u)
            vs = [product(tok, grad, row, col, k + i) for i in range(2)]
            encode(vs, out, pl.multiple_of((n * UNITS + u) * PAIR, 16))
            return 0

        lax.fori_loop(0, UNITS, body, 0, unroll=UNROLL)


def second_kernel(steps, row, col, where, tok, grad, recv, *rest):
    y, x, core = place(where[0])
    half_units = UNITS // 2

    def run(n, step, first, out, relay):
        def body(i, _):
            u = first + i
            k = block_of(core, y, x, step, u)
            got = decode(recv, pl.multiple_of((n * UNITS + u) * PAIR, 16), 2)
            vs = [product(tok, grad, row, col, k + i) + got[i] for i in range(2)]
            if relay is not None:
                more = decode(relay, pl.multiple_of(i * PAIR, 16), 2)
                vs = [a + b for a, b in zip(vs, more)]
            at = u if step != 2 else i
            if step:
                encode(vs, out, pl.multiple_of(at * PAIR, 16))
            else:
                for j in range(2):
                    out[pl.ds(pl.multiple_of((at * 2 + j) * BS, BS), BS), :] = vs[j]
            return 0

        lax.fori_loop(0, half_units, body, 0, unroll=UNROLL)

    if steps == (2,):
        run(0, 2, 0, rest[0], None)
        run(0, 2, half_units, rest[1], None)
    elif steps == (0,):
        run(0, 0, 0, rest[0], None)
        run(0, 0, half_units, rest[0], None)
    else:
        from_back, from_front, on, back = rest
        run(0, 1, half_units, on, None)
        run(1, 3, 0, back, None)
        run(0, 1, 0, on, from_back)
        run(1, 3, half_units, back, from_front)


def third_kernel(where, own, r1, r3, m1, m2, m3, keep):
    y, x, core = place(where[0])
    here = jnp.where(core == 0, x, y)
    for step, out in ((2, m2), (1, m1), (3, m3), (0, keep)):

        def body(n, _, step=step, out=out):
            u = lax.rem(here + step, SIDE) * 4 + n
            base = pl.multiple_of(u * PAIR, 16)
            got = [decode(r, base, 2) for r in (r1, r3)]
            vs = []
            for i in range(2):
                v = own[pl.ds(pl.multiple_of((u * 2 + i) * BS, BS), BS), :]
                vs.append(v + (got[0][i] + got[1][i]))
            if step:
                encode(vs, out, pl.multiple_of(n * PAIR, 16))
            else:
                for i in range(2):
                    out[pl.ds(pl.multiple_of((n * 2 + i) * BS, BS), BS), :] = vs[i]
            return 0

        lax.fori_loop(0, 4, body, 0, unroll=2)


def plane_kernel(where, own, r1, r2, r3, mine, other):
    _, _, core = place(where[0])
    for cc, out in ((core, mine), (1 - core, other)):
        for jp in range(2):
            u = cc * 2 + jp
            got = [decode(r, pl.multiple_of(u * PAIR, 16), 2) for r in (r1, r2, r3)]
            for i in range(2):
                v = own[pl.ds(pl.multiple_of((u * 2 + i) * BS, BS), BS), :]
                out[jp * 2 + i] = v + (got[0][i] + got[1][i]) + got[2][i]


def fourth_kernel(reps, slots, where, lists, mine, other, keep, out, sums):
    z = where[1]
    _, _, core = place(where[0])
    for i in range(4):
        sums[core * 4 + i] = mine[i]
        sums[(1 - core) * 4 + i] = other[i]
    sums[8] = jnp.zeros((BS, BS), jnp.float32)

    def body(p, _):
        encode([sums[lists[p * slots + t]] for t in range(slots)], out.at[p], 0)
        return 0

    lax.fori_loop(0, reps, body, 0, unroll=2)
    for t in range(slots):
        keep[pl.ds(t * BS, BS), :] = sums[lists[z * slots + t]]


def fifth_kernel(scale, reps, slots, where, own, recv, out):
    for t in range(slots):
        out[t] = own[pl.ds(t * BS, BS), :]

    def body(shift, _):
        got = decode(recv.at[lax.rem(where[1] + shift, reps)], 0, slots)
        for t in range(slots):
            out[t] += got[t]
        return 0

    lax.fori_loop(1, reps, body, 0)
    for t in range(slots):
        out[t] = out[t] * scale


def token_kernel(row, col, where, grad, *rest):
    pieces, out, acc = rest[:-2], rest[-2], rest[-1]
    y, x, core = place(where[0])
    acc[...] = jnp.zeros_like(acc)
    for n, piece in enumerate(pieces):
        half = core if n < 5 else 1 - core
        back, first = ((0, 0), (1, 0), (3, 0), (2, 0), (2, 4 * SIDE))[n % 5]

        def body(at, _, piece=piece, half=half, back=back, first=first):
            i = first + at
            other = lax.div(i, 8)
            yy = jnp.where(half == 0, back, other)
            xx = jnp.where(half == 0, other, back)
            chip = lax.rem(y + SIDE - yy, SIDE) * SIDE + lax.rem(x + SIDE - xx, SIDE)
            owner = lax.rem(half + lax.rem(lax.div(i, 4), 2), 2)
            k = (chip * CORES + owner) * 8 + half * 4 + lax.rem(i, 4)
            left = grad[:, pl.ds(pl.multiple_of(col[k] * BS, BS), BS)]
            part = lax.dot_general(
                left,
                piece[pl.ds(pl.multiple_of(at * BS, BS), BS), :],
                (((1,), (1,)), ((), ())),
                preferred_element_type=jnp.float32,
            )
            acc[:, pl.ds(pl.multiple_of(row[k] * BS, BS), BS)] += part
            return 0

        lax.fori_loop(0, piece.shape[0] // BS, body, 0, unroll=4)
    out[...] = acc[...].astype(jnp.bfloat16)


def call(kernel, in_specs, outs, *args, scratch=(), flops=0, moved=0, limit=16):
    return pl.pallas_call(
        kernel,
        in_specs=in_specs,
        out_specs=[VMEM] * len(outs),
        out_shape=outs,
        scratch_shapes=list(scratch),
        compiler_params=pltpu.CompilerParams(vmem_limit_bytes=limit * 1024 * 1024),
        cost_estimate=pl.CostEstimate(flops=flops, bytes_accessed=moved, transcendentals=0),
    )(*args)


def move(a, axis, pairs):
    return lax.ppermute(a, axis, pairs)


def work(tokens, out_grad, weight_blocks, block_row, block_col, send_list):
    fsdp = lax.axis_size("fsdp")
    reps = lax.axis_size("rep")
    slots = send_list.shape[2]
    rows_here = tokens.shape[0]
    nnz = block_row.shape[0]
    scale = float(rows_here * reps * fsdp) ** -0.5
    where = jnp.stack([lax.axis_index("fsdp"), lax.axis_index("rep")]).astype(jnp.int32)

    def ring(first, step):
        pairs = []
        for f in range(fsdp):
            y, x, c = f // (SIDE * CORES), f // CORES % SIDE, f % CORES
            dy, dx = (step, 0) if (c == 0) == first else (0, step)
            to = ((y + dy) % SIDE * SIDE + (x + dx) % SIDE) * CORES + c
            pairs.append((f, to))
        return pairs

    swap = [(f, f ^ 1) for f in range(fsdp)]
    group_shape = jax.ShapeDtypeStruct((UNITS * PAIR, BS), jnp.bfloat16)
    kept_shape = jax.ShapeDtypeStruct((UNITS * 2 * BS, BS), jnp.float32)

    core = lax.rem(lax.axis_index("fsdp"), CORES)
    flat = weight_blocks.reshape(8 * BS, BS)
    stay = lax.dynamic_slice_in_dim(flat, core * 4 * BS, 4 * BS, 0)
    leave = lax.dynamic_slice_in_dim(flat, (1 - core) * 4 * BS, 4 * BS, 0)
    part = jnp.concatenate([stay, move(leave, "fsdp", swap)], axis=0)
    along = [part] + [move(part, "fsdp", ring(False, s)) for s in (1, 2, 3)]
    along = jnp.concatenate(along, axis=0)
    back, front = (move(along, "fsdp", ring(True, s)) for s in (1, 3))
    middle = along.shape[0] // 2
    far = [move(back[:middle], "fsdp", ring(True, 1)), move(front[middle:], "fsdp", ring(True, 3))]
    pieces = [along, back, front, *far]
    pieces += [move(p, "fsdp", swap) for p in pieces]

    tok = fast(tokens.T)
    grad = fast(out_grad)
    flops = 2 * rows_here * BS * BS * 32
    order = ((2,), (1, 3), (0,))
    arrived = []
    for steps in order:
        mine = call(
            functools.partial(first_kernel, steps),
            [SMEM, SMEM, SMEM, VMEM, VMEM],
            [jax.ShapeDtypeStruct((len(steps) * UNITS * PAIR, BS), jnp.bfloat16)],
            block_row, block_col, where, tok, grad,
            flops=flops * len(steps),
        )[0]
        arrived.append(move(mine, "fsdp", swap))
    half_shape = jax.ShapeDtypeStruct((UNITS // 2 * PAIR, BS), jnp.bfloat16)

    def second(i, outs, *more):
        steps = order[i]
        return call(
            functools.partial(second_kernel, steps),
            [SMEM, SMEM, SMEM] + [VMEM] * (3 + len(more)),
            outs,
            block_row, block_col, where, tok, grad, arrived[i], *more,
            flops=flops * len(steps),
        )

    on, behind = second(0, [half_shape] * 2)
    from_back = move(on, "fsdp", ring(True, 1))
    from_front = move(behind, "fsdp", ring(True, 3))
    (kept,) = second(2, [kept_shape])
    on, behind = second(1, [group_shape] * 2, from_back, from_front)
    recv = {1: move(on, "fsdp", ring(True, 1)), 3: move(behind, "fsdp", ring(True, 3))}
    small = jax.ShapeDtypeStruct((4 * PAIR, BS), jnp.bfloat16)
    m1, m2, m3, keep = call(
        third_kernel,
        [SMEM] + [VMEM] * 3,
        [small] * 3 + [jax.ShapeDtypeStruct((8 * BS, BS), jnp.float32)],
        where, kept, recv[1], recv[3],
    )
    got = {s: move(m, "fsdp", ring(False, s)) for s, m in ((2, m2), (1, m1), (3, m3))}
    mine, other = call(
        plane_kernel,
        [SMEM] + [VMEM] * 4,
        [jax.ShapeDtypeStruct((4, BS, BS), jnp.float32)] * 2,
        where, keep, got[1], got[2], got[3],
    )
    other = move(other, "fsdp", swap)
    zrows = slots * BS + SIDEBAND
    keep, outgoing = call(
        functools.partial(fourth_kernel, reps, slots),
        [SMEM, SMEM] + [VMEM] * 2,
        [
            jax.ShapeDtypeStruct((slots * BS, BS), jnp.float32),
            jax.ShapeDtypeStruct((reps, zrows, BS), jnp.bfloat16),
        ],
        where, send_list.reshape(-1), mine, other,
        scratch=[pltpu.VMEM((9, BS, BS), jnp.float32)],
    )
    incoming = lax.all_to_all(outgoing, "rep", split_axis=0, concat_axis=0, tiled=True)
    token_grad = call(
        token_kernel,
        [SMEM, SMEM, SMEM] + [VMEM] * 11,
        [jax.ShapeDtypeStruct(tokens.shape, jnp.bfloat16)],
        block_row, block_col, where, grad, *pieces,
        scratch=[pltpu.VMEM(tokens.shape, jnp.float32)],
        flops=2 * rows_here * BS * BS * nnz,
        limit=20,
    )[0]
    incoming, token_grad = lax.optimization_barrier((incoming, token_grad))
    grad_owned = call(
        functools.partial(fifth_kernel, scale, reps, slots),
        [SMEM, VMEM, VMEM],
        [jax.ShapeDtypeStruct((slots, BS, BS), jnp.float32)],
        where, keep, incoming,
    )[0]
    return token_grad, grad_owned[None, None]


def solution(mesh):
    return jax.shard_map(
        work,
        mesh=mesh,
        in_specs=(
            P(("rep", "fsdp"), None),
            P(("rep", "fsdp"), None),
            P("fsdp", None, None),
            P(),
            P(),
            P("fsdp", None, None),
        ),
        out_specs=(P(("rep", "fsdp"), None), P("rep", "fsdp", None, None, None)),
        check_vma=False,
    )
```

time: 344 us -> 142 us (0.41)
  waiting for transfers between devices: 177 us -> 36.3 us
  matrix products: 85.4 us -> 0 us
  Pallas kernels: 0 us -> 56.4 us
  local copies, waits for them, and re-layouts: 53.3 us -> 17.4 us
  starting transfers between devices: 6.82 us -> 30.3 us
  between operations: 14.1 us -> 0.86 us
  other arithmetic: 6.41 us -> 0.1 us
    reduce_scatter x1 -> x0, waiting for transfers between devices: 124 us -> none  [local(): lax.psum_scatter(block_sums(features, grad_cols, block_row, block_col), '...]
    dot_general x3 -> x0, matrix products: 85.4 us -> none  [the longest x1 45.6 us: spread(): jnp.einsum('tnk,nq->tqk', products, chosen, precision=lax.Precision.HIGHEST)]
    pallas_call x0 -> x11, Pallas kernels: none -> 56.4 us  [call(): pl.pallas_call(kernel, in_specs=in_specs, out_specs=[VMEM] * len(outs), o...]
    all_gather x1 -> x0, waiting for transfers between devices: 51.8 us -> none  [local(): all_blocks = lax.all_gather(weight_blocks, 'fsdp', axis=0, tiled=True)]
    ppermute x0 -> x24, waiting for transfers between devices: none -> 36.3 us  [move(): return lax.ppermute(a, axis, pairs)]
    gather x3 -> x0, local copies, waits for them, and re-layouts: 23.3 us -> none  [the longest x1 12.9 us: block_products(): picked = jnp.take(grad_cols, col_ids, axis=1)]
    ppermute x0 -> x24, starting transfers between devices: none -> 22.9 us  [move(): return lax.ppermute(a, axis, pairs)]
    reshape x2 -> x1, local copies, waits for them, and re-layouts: 13.7 us -> 0.08 us  [work(): send_list.reshape(-1)]
  transfers between devices with their start and end apart: 3 -> 25, of which waited for: 2 -> 10; matrix products, arithmetic and copies ran while one was open for 21% -> 3% of each run, Pallas kernels for 0% -> 34%
where the time goes in v1:
time: 142 us; the launch traced here: 141 us
  Pallas kernels  56.4 us (40%)
  waiting for transfers between devices  36.3 us (26%)
  starting transfers between devices  30.3 us (21%)
  local copies, waits for them, and re-layouts  17.4 us (12%)
    pallas_call x11, Pallas kernels, call(): pl.pallas_call(kernel, in_specs=in_specs, out_specs=[VMEM] * len(outs), o...  56.4 us
    ppermute x24, waiting for transfers between devices, move(): return lax.ppermute(a, axis, pairs)  36.3 us
    ppermute x24, starting transfers between devices, move(): return lax.ppermute(a, axis, pairs)  22.9 us
    unnamed x20, local copies, waits for them, and re-layouts  15.5 us
    all_to_all x1, starting transfers between devices, work(): lax.all_to_all(outgoing, 'rep', split_axis=0, concat_axis=0, tiled=True)  7.38 us
  transfers between devices with their start and end apart: 25, of which 10 were waited for; matrix products, arithmetic and copies ran while one was open for 3% of the time, Pallas kernels for 34%

profile of v1, /device:TPU:1, one launch (start us, length us, event | category | flops | bytes accessed | tf_op | source)
XLA Modules:
  0.0 141.4 jit_solution(10290652052573323792)
XLA Ops:
  0.7 3.3 %copy.11 = bf16[256,4096]{0,1:T(8,128)(2,1)S(1)} copy(bf16[256,4096]{1,0:T(8,128)(2,1)} %param.6) | data formatting | bytes 4194304 | tf_op args[0]
  3.9 0.1 pad_add_fusion.where
  4.0 3.1 %copy-done = bf16[256,14336]{1,0:T(8,128)(2,1)S(1)} copy-done((bf16[256,14336]{1,0:T(8,128)(2,1)S(1)}, bf16[256,14336]{1,0:T(8,128)(2,1)}, u32[]{:S(2)}) %copy-start) | copy-done | bytes 7340056
  7.1 6.9 %shard_map.79 = bf16[8704,128]{1,0:T(8,128)(2,1)} custom-call(s32[256]{0:T(256)S(1)} %copy-done.3, s32[256]{0:T(256)S(1)} %copy-done.4, s32[2]{0:T(128)S(1)} %pad_add_fusion.where, bf16[4096,256]{1,0:T(8,128)(2,1)S(1)} %bitcast.5, bf16[256,14336]{1,0:T(8,128)(2,1)S(1)} %copy-done), custom_call_target="tpu_custom_call" | custom-call | flops 536870912 | tf_op jit(solution)/shard_map/pallas_call | solution.py:221
  14.1 3.2 %collective-permute-start.1 = (bf16[8704,128]{1,0:T(8,128)(2,1)}, bf16[8704,128]{1,0:T(8,128)(2,1)}, u32[]{:S(2)}, u32[]{:S(2)}) collective-permute-start(bf16[8704,128]{1,0:T(8,128)(2,1)} %shard_map.79), channel_id=1, source_target_pairs={{0,1},{1,0},{2,3},{3,2},{4,5},{5,4},{6,7},{7,6},{8,9},{9,8},{10,11... | collective-permute-start | bytes 6684680 | tf_op jit(solution)/shard_map/ppermute | solution.py:233
  17.3 3.0 %shard_map.80 = bf16[4352,128]{1,0:T(8,128)(2,1)S(1)} custom-call(s32[256]{0:T(256)S(1)} %copy-done.3, s32[256]{0:T(256)S(1)} %copy-done.4, s32[2]{0:T(128)S(1)} %pad_add_fusion.where, bf16[4096,256]{1,0:T(8,128)(2,1)S(1)} %bitcast.6, bf16[256,14336]{1,0:T(8,128)(2,1)S(1)} %copy-done), custom_call_target="tpu_custom_call" | custom-call | flops 268435456 | tf_op jit(solution)/shard_map/pallas_call | solution.py:221
  20.3 0.0 copy-start.5
  20.3 0.1 collective-permute-start.2
  20.4 2.7 %collective-permute-done.2.recv = bf16[4352,128]{1,0:T(8,128)(2,1)S(1)} collective-permute-done((bf16[4352,128]{1,0:T(8,128)(2,1)S(1)}, bf16[4352,128]{1,0:T(8,128)(2,1)S(1)}, u32[]{:S(2)}, u32[]{:S(2)}) %collective-permute-start.2) | collective-permute-done | bytes 1114144 | tf_op jit(solution)/shard_map/ppermute | solution.py:233
  23.1 4.1 %shard_map.81 = (bf16[2176,128]{1,0:T(8,128)(2,1)}, bf16[2176,128]{1,0:T(8,128)(2,1)}) custom-call(s32[256]{0:T(256)S(1)} %copy-done.3, s32[256]{0:T(256)S(1)} %copy-done.4, s32[2]{0:T(128)S(1)} %pad_add_fusion.where, bf16[4096,256]{1,0:T(8,128)(2,1)S(1)} %bitcast.7, bf16[256,14336]{1,0:T(8,128)(2,1)S(1)} %copy-done, ...), custom_call_target="tpu_custom_call" | custom-call | flops 268435456 | tf_op jit(solution)/shard_map/pallas_call | solution.py:221
  27.3 0.0 collective-permute-start.3
  27.3 2.7 %collective-permute-start.4 = (bf16[2176,128]{1,0:T(8,128)(2,1)}, bf16[2176,128]{1,0:T(8,128)(2,1)S(1)}, u32[]{:S(2)}, u32[]{:S(2)}) collective-permute-start(bf16[2176,128]{1,0:T(8,128)(2,1)} %get-tuple-element.17), channel_id=1, source_target_pairs={{0,24},{1,7},{2,26},{3,1},{4,28},{5,3},{6,30},{7,5},{8,0},{9,15},{... | collective-permute-start | bytes 1671176 | tf_op jit(solution)/shard_map/ppermute | solution.py:233
  29.9 0.7 constant_dynamic-update-slice_fusion.4
  30.6 0.9 collective-permute-start.11
  31.5 3.1 %copy-done.1 = bf16[256,14336]{1,0:T(8,128)(2,1)S(1)} copy-done((bf16[256,14336]{1,0:T(8,128)(2,1)S(1)}, bf16[256,14336]{1,0:T(8,128)(2,1)}, u32[]{:S(2)}) %copy-start.1) | copy-done | bytes 7340056
  34.6 3.0 %shard_map.77 = bf16[4352,128]{1,0:T(8,128)(2,1)S(1)} custom-call(s32[256]{0:T(256)S(1)} %copy-done.3, s32[256]{0:T(256)S(1)} %copy-done.4, s32[2]{0:T(128)S(1)} %pad_add_fusion.where, bf16[4096,256]{1,0:T(8,128)(2,1)S(1)} %bitcast.8, bf16[256,14336]{1,0:T(8,128)(2,1)S(1)} %copy-done.1), custom_call_target="tpu_custom_call" | custom-call | flops 268435456 | tf_op jit(solution)/shard_map/pallas_call | solution.py:221
  37.6 0.1 collective-permute-start
  37.7 0.0 collective-permute-done.3.rest_0_
  37.8 7.5 %shard_map.82 = (bf16[4352,128]{1,0:T(8,128)(2,1)S(1)}, bf16[4352,128]{1,0:T(8,128)(2,1)S(1)}) custom-call(s32[256]{0:T(256)S(1)} %copy-done.3, s32[256]{0:T(256)S(1)} %copy-done.4, s32[2]{0:T(128)S(1)} %pad_add_fusion.where, bf16[4096,256]{1,0:T(8,128)(2,1)S(1)} %bitcast.9, bf16[256,14336]{1,0:T(8,128)(2,1)S(1)} %copy-done.1, ...), custom_call_target="tpu_custom_call" | custom-call | flops 536870912 | tf_op jit(solution)/shard_map/pallas_call | solution.py:221
  45.3 0.1 collective-permute-start.5
  45.4 2.7 %collective-permute-start.6 = (bf16[4352,128]{1,0:T(8,128)(2,1)S(1)}, bf16[4352,128]{1,0:T(8,128)(2,1)S(1)}, u32[]{:S(2)}, u32[]{:S(2)}) collective-permute-start(bf16[4352,128]{1,0:T(8,128)(2,1)S(1)} %get-tuple-element.19), channel_id=1, source_target_pairs={{0,24},{1,7},{2,26},{3,1},{4,28},{5,3},{6,30},{7,5},{8,0},{9,15},{... | collective-permute-start | bytes 3342344 | tf_op jit(solution)/shard_map/ppermute | solution.py:233
  48.1 0.1 collective-permute-start.12
  48.2 1.9 %collective-permute-start.13 = (bf16[1024,128]{1,0:T(8,128)(2,1)S(1)}, bf16[1024,128]{1,0:T(8,128)(2,1)S(1)}, u32[]{:S(2)}, u32[]{:S(2)}) collective-permute-start(bf16[1024,128]{1,0:T(8,128)(2,1)S(1)} %pad_maximum_fusion), channel_id=1, source_target_pairs={{0,4},{1,17},{2,6},{3,19},{4,0},{5,21},{6,2},{7,23},{8,12},{9,25},... | collective-permute-start | bytes 786440 | tf_op jit(solution)/shard_map/ppermute | solution.py:233
  50.0 9.2 %collective-permute-done.12 = bf16[1024,128]{1,0:T(8,128)(2,1)S(1)} collective-permute-done((bf16[1024,128]{1,0:T(8,128)(2,1)S(1)}, bf16[1024,128]{1,0:T(8,128)(2,1)S(1)}, u32[]{:S(2)}, u32[]{:S(2)}) %collective-permute-start.12) | collective-permute-done | bytes 262176 | tf_op jit(solution)/shard_map/ppermute | solution.py:233
  59.2 0.7 constant_dynamic-update-slice_fusion.3
  59.9 0.7 constant_dynamic-update-slice_fusion.2
  60.6 1.2 collective-permute-done.13
  61.8 0.7 constant_dynamic-update-slice_fusion.1
  62.5 4.5 %collective-permute-done.14 = bf16[1024,128]{1,0:T(8,128)(2,1)S(1)} collective-permute-done((bf16[1024,128]{1,0:T(8,128)(2,1)S(1)}, bf16[1024,128]{1,0:T(8,128)(2,1)S(1)}, u32[]{:S(2)}, u32[]{:S(2)}) %collective-permute-start.14) | collective-permute-done | bytes 262176 | tf_op jit(solution)/shard_map/ppermute | solution.py:233
  67.1 0.7 constant_dynamic-update-slice_fusion.rest_0_
  67.8 0.0 collective-permute-start.15
  67.8 2.7 %collective-permute-start.16 = (bf16[4096,128]{1,0:T(8,128)(2,1)}, bf16[4096,128]{1,0:T(8,128)(2,1)}, u32[]{:S(2)}, u32[]{:S(2)}) collective-permute-start(bf16[4096,128]{1,0:T(8,128)(2,1)} %constant_dynamic-update-slice_fusion.rest_0_), channel_id=1, source_target_pairs={{0,24},{1,7},{2,26},{3,1},{4,28},{5,3},{6,30},{7,5},{8,0},{9,15},{... | collective-permute-start | bytes 3145736 | tf_op jit(solution)/shard_map/ppermute | solution.py:233
  70.5 0.0 collective-permute-done.recv
  70.5 2.8 %shard_map.78.own = f32[4096,128]{1,0:T(8,128)S(1)} custom-call(s32[256]{0:T(256)S(1)} %copy-done.3, s32[256]{0:T(256)S(1)} %copy-done.4, s32[2]{0:T(128)S(1)} %pad_add_fusion.where, bf16[4096,256]{1,0:T(8,128)(2,1)S(1)} %bitcast.10, bf16[256,14336]{1,0:T(8,128)(2,1)S(1)} %copy-done.1, bf16[4352,128]{1,0:T(8,128)(2,1)S(1)} %collective-permute-done.recv), custom_call_target="tpu_custom_call" | custom-call | flops 268435456 | tf_op jit(solution)/shard_map/pallas_call | solution.py:221
  73.3 2.5 %shard_map.83 = (bf16[1088,128]{1,0:T(8,128)(2,1)S(1)}, bf16[1088,128]{1,0:T(8,128)(2,1)S(1)}, bf16[1088,128]{1,0:T(8,128)(2,1)S(1)}, f32[1024,128]{1,0:T(8,128)S(1)}) custom-call(s32[2]{0:T(128)S(1)} %pad_add_fusion.where, f32[4096,128]{1,0:T(8,128)S(1)} %shard_map.78.own, bf16[4352,128]{1,0:T(8,128)(2,1)S(1)} %collective-permute-done.5.r1, ...), custom_call_target="tpu_custom_call" | custom-call | tf_op jit(solution)/shard_map/pallas_call | solution.py:221
  75.8 0.0 copy-start.6
  75.8 0.1 collective-permute-start.7
  75.9 2.8 %collective-permute-start.8 = (bf16[1088,128]{1,0:T(8,128)(2,1)S(1)}, bf16[1088,128]{1,0:T(8,128)(2,1)S(1)}, u32[]{:S(2)}, u32[]{:S(2)}) collective-permute-start(bf16[1088,128]{1,0:T(8,128)(2,1)S(1)} %get-tuple-element.22), channel_id=1, source_target_pairs={{0,4},{1,17},{2,6},{3,19},{4,0},{5,21},{6,2},{7,23},{8,12},{9,25},... | collective-permute-start | bytes 835592 | tf_op jit(solution)/shard_map/ppermute | solution.py:233
  78.7 7.1 %collective-permute-done.7.r1 = bf16[1088,128]{1,0:T(8,128)(2,1)S(1)} collective-permute-done((bf16[1088,128]{1,0:T(8,128)(2,1)S(1)}, bf16[1088,128]{1,0:T(8,128)(2,1)S(1)}, u32[]{:S(2)}, u32[]{:S(2)}) %collective-permute-start.7) | collective-permute-done | bytes 278560 | tf_op jit(solution)/shard_map/ppermute | solution.py:233
  85.8 3.7 %collective-permute-done.8.r2 = bf16[1088,128]{1,0:T(8,128)(2,1)S(1)} collective-permute-done((bf16[1088,128]{1,0:T(8,128)(2,1)S(1)}, bf16[1088,128]{1,0:T(8,128)(2,1)S(1)}, u32[]{:S(2)}, u32[]{:S(2)}) %collective-permute-start.8) | collective-permute-done | bytes 278560 | tf_op jit(solution)/shard_map/ppermute | solution.py:233
  89.4 0.0 collective-permute-done.9.r3
  89.4 1.1 shard_map.84
  90.5 0.2 collective-permute-start.10
  90.7 0.1 copy.10
  90.8 0.1 reshape.10.lists
  90.9 1.3 collective-permute-done.10.other
  92.1 1.9 %shard_map.85 = (f32[384,128]{1,0:T(8,128)S(1)}, bf16[8,400,128]{2,1,0:T(8,128)(2,1)}) custom-call(s32[2]{0:T(128)S(1)} %pad_add_fusion.where, s32[24]{0:T(128)S(1)} %reshape.10.lists, f32[4,128,128]{2,1,0:T(8,128)S(1)} %get-tuple-element.24.mine, f32[4,128,128]{2,1,0:T(8,128)S(1)} %collective-permute-done.10.other), custom_call_target="tpu_custom_call" | custom-call | tf_op jit(solution)/shard_map/pallas_call | solution.py:221
  94.0 7.4 %all-to-all-start = ((bf16[8,400,128]{2,1,0:T(8,128)(2,1)}), bf16[8,400,128]{2,1,0:T(8,128)(2,1)S(1)}, u32[]{:S(2)}, u32[]{:S(2)}) async-start(bf16[8,400,128]{2,1,0:T(8,128)(2,1)} %get-tuple-element.26), calls=%async_computation | async-start | bytes 1638400 | tf_op jit(solution)/shard_map/all_to_all | solution.py:329
  101.4 0.4 collective-permute-start.19
  101.9 0.1 collective-permute-start.17
  102.0 1.1 slice.9
  103.1 2.7 %collective-permute-start.18 = (bf16[2048,128]{1,0:T(8,128)(2,1)S(1)}, bf16[2048,128]{1,0:T(8,128)(2,1)S(1)}, u32[]{:S(2)}, u32[]{:S(2)}) collective-permute-start(bf16[2048,128]{1,0:T(8,128)(2,1)S(1)} %slice.9), channel_id=1, source_target_pairs={{0,24},{1,7},{2,26},{3,1},{4,28},{5,3},{6,30},{7,5},{8,0},{9,15},{... | collective-permute-start | bytes 1572872 | tf_op jit(solution)/shard_map/ppermute | solution.py:233
  105.8 0.7 collective-permute-start.20
  106.4 0.0 collective-permute-start.21
  106.4 5.0 %collective-permute-done.17.rest_3_ = bf16[2048,128]{1,0:T(8,128)(2,1)S(1)} collective-permute-done((bf16[2048,128]{1,0:T(8,128)(2,1)S(1)}, bf16[2048,128]{1,0:T(8,128)(2,1)S(1)}, u32[]{:S(2)}, u32[]{:S(2)}) %collective-permute-start.17) | collective-permute-done | bytes 524320 | tf_op jit(solution)/shard_map/ppermute | solution.py:233
  111.5 0.9 collective-permute-start.22
  112.4 0.0 collective-permute-done.18.rest_4_
  112.4 0.7 collective-permute-start.23
  113.1 0.8 collective-permute-done.22.rest_8_
  114.0 0.7 collective-permute-done.23.rest_9_
  114.7 0.0 collective-permute-done.21.rest_7_
  114.7 3.1 %copy-done.2 = bf16[256,14336]{1,0:T(8,128)(2,1)S(1)} copy-done((bf16[256,14336]{1,0:T(8,128)(2,1)S(1)}, bf16[256,14336]{1,0:T(8,128)(2,1)}, u32[]{:S(2)}) %copy-start.2) | copy-done | bytes 7340056
  117.8 21.7 %shard_map.86 = bf16[256,4096]{1,0:T(8,128)(2,1)} custom-call(s32[256]{0:T(256)S(1)} %copy-done.3, s32[256]{0:T(256)S(1)} %copy-done.4, s32[2]{0:T(128)S(1)} %pad_add_fusion.where, bf16[256,14336]{1,0:T(8,128)(2,1)S(1)} %copy-done.2, bf16[4096,128]{1,0:T(8,128)(2,1)} %constant_dynamic-update-slice_fusion.rest_0_, ...), custom_call_target="tpu_custom_call" | custom-call | flops 2147483648 | tf_op jit(solution)/shard_map/pallas_call | solution.py:221
  139.6 1.8 %shard_map.87 = f32[3,128,128]{2,1,0:T(8,128)} custom-call(s32[2]{0:T(128)S(1)} %pad_add_fusion.where, f32[384,128]{1,0:T(8,128)S(1)} %get-tuple-element.28.own, bf16[8,400,128]{2,1,0:T(8,128)(2,1)S(1)} %all-to-all-done.recv), custom_call_target="tpu_custom_call" | custom-call | tf_op jit(solution)/shard_map/pallas_call | solution.py:221
  (23 shorter events, 0.1 us)
Async XLA Ops:
  0.6 3.4 %copy-start.3 = (s32[256]{0:T(256)S(1)}, s32[256]{0:T(256)}, u32[]{:S(2)}) copy-start(s32[256]{0:T(256)} %row.13) | copy-start | bytes 3076
  0.6 3.4 %copy-start.4 = (s32[256]{0:T(256)S(1)}, s32[256]{0:T(256)}, u32[]{:S(2)}) copy-start(s32[256]{0:T(256)} %col.13) | copy-start | bytes 3076
  4.0 3.1 %copy-start = (bf16[256,14336]{1,0:T(8,128)(2,1)S(1)}, bf16[256,14336]{1,0:T(8,128)(2,1)}, u32[]{:S(2)}) copy-start(bf16[256,14336]{1,0:T(8,128)(2,1)} %grad.13) | copy-start | bytes 22020100
  14.1 23.7 %collective-permute-start.1 = (bf16[8704,128]{1,0:T(8,128)(2,1)}, bf16[8704,128]{1,0:T(8,128)(2,1)}, u32[]{:S(2)}, u32[]{:S(2)}) collective-permute-start(bf16[8704,128]{1,0:T(8,128)(2,1)} %shard_map.79), channel_id=1, source_target_pairs={{0,1},{1,0},{2,3},{3,2},{4,5},{5,4},{6,7},{7,6},{8,9},{9,8},{10,11... | collective-permute-start | bytes 6684680 | tf_op jit(solution)/shard_map/ppermute | solution.py:233
  20.3 9.6 %copy-start.5 = (bf16[8,128,128]{2,1,0:T(8,128)(2,1)S(1)}, bf16[8,128,128]{2,1,0:T(8,128)(2,1)}, u32[]{:S(2)}) copy-start(bf16[8,128,128]{2,1,0:T(8,128)(2,1)} %param.8) | copy-start | bytes 786436
  20.3 2.8 %collective-permute-start.2 = (bf16[4352,128]{1,0:T(8,128)(2,1)S(1)}, bf16[4352,128]{1,0:T(8,128)(2,1)S(1)}, u32[]{:S(2)}, u32[]{:S(2)}) collective-permute-start(bf16[4352,128]{1,0:T(8,128)(2,1)S(1)} %shard_map.80), channel_id=1, source_target_pairs={{0,1},{1,0},{2,3},{3,2},{4,5},{5,4},{6,7},{7,6},{8,9},{9,8},{10,11... | collective-permute-start | bytes 3342344 | tf_op jit(solution)/shard_map/ppermute | solution.py:233
  27.3 10.5 %collective-permute-start.3 = (bf16[2176,128]{1,0:T(8,128)(2,1)}, bf16[2176,128]{1,0:T(8,128)(2,1)S(1)}, u32[]{:S(2)}, u32[]{:S(2)}) collective-permute-start(bf16[2176,128]{1,0:T(8,128)(2,1)} %get-tuple-element.16), channel_id=1, source_target_pairs={{0,8},{1,3},{2,10},{3,5},{4,12},{5,7},{6,14},{7,1},{8,16},{9,11},{... | collective-permute-start | bytes 1671176 | tf_op jit(solution)/shard_map/ppermute | solution.py:233
  27.3 10.5 %collective-permute-start.4 = (bf16[2176,128]{1,0:T(8,128)(2,1)}, bf16[2176,128]{1,0:T(8,128)(2,1)S(1)}, u32[]{:S(2)}, u32[]{:S(2)}) collective-permute-start(bf16[2176,128]{1,0:T(8,128)(2,1)} %get-tuple-element.17), channel_id=1, source_target_pairs={{0,24},{1,7},{2,26},{3,1},{4,28},{5,3},{6,30},{7,5},{8,0},{9,15},{... | collective-permute-start | bytes 1671176 | tf_op jit(solution)/shard_map/ppermute | solution.py:233
  30.6 17.4 %collective-permute-start.11 = (bf16[512,128]{1,0:T(8,128)(2,1)S(1)}, bf16[512,128]{1,0:T(8,128)(2,1)S(1)}, u32[]{:S(2)}, u32[]{:S(2)}) collective-permute-start(bf16[512,128]{1,0:T(8,128)(2,1)S(1)} %get-tuple-element.32), channel_id=1, source_target_pairs={{0,1},{1,0},{2,3},{3,2},{4,5},{5,4},{6,7},{7,6},{8,9},{9,8},{10,11... | collective-permute-start | bytes 393224 | tf_op jit(solution)/shard_map/ppermute | solution.py:233
  31.5 3.1 %copy-start.1 = (bf16[256,14336]{1,0:T(8,128)(2,1)S(1)}, bf16[256,14336]{1,0:T(8,128)(2,1)}, u32[]{:S(2)}) copy-start(bf16[256,14336]{1,0:T(8,128)(2,1)} %grad.13) | copy-start | bytes 22020100
  37.6 32.9 %collective-permute-start = (bf16[4352,128]{1,0:T(8,128)(2,1)S(1)}, bf16[4352,128]{1,0:T(8,128)(2,1)S(1)}, u32[]{:S(2)}, u32[]{:S(2)}) collective-permute-start(bf16[4352,128]{1,0:T(8,128)(2,1)S(1)} %shard_map.77), channel_id=1, source_target_pairs={{0,1},{1,0},{2,3},{3,2},{4,5},{5,4},{6,7},{7,6},{8,9},{9,8},{10,11... | collective-permute-start | bytes 3342344 | tf_op jit(solution)/shard_map/ppermute | solution.py:233
  45.3 28.0 %collective-permute-start.5 = (bf16[4352,128]{1,0:T(8,128)(2,1)S(1)}, bf16[4352,128]{1,0:T(8,128)(2,1)S(1)}, u32[]{:S(2)}, u32[]{:S(2)}) collective-permute-start(bf16[4352,128]{1,0:T(8,128)(2,1)S(1)} %get-tuple-element.18), channel_id=1, source_target_pairs={{0,8},{1,3},{2,10},{3,5},{4,12},{5,7},{6,14},{7,1},{8,16},{9,11},{... | collective-permute-start | bytes 3342344 | tf_op jit(solution)/shard_map/ppermute | solution.py:233
  45.4 27.9 %collective-permute-start.6 = (bf16[4352,128]{1,0:T(8,128)(2,1)S(1)}, bf16[4352,128]{1,0:T(8,128)(2,1)S(1)}, u32[]{:S(2)}, u32[]{:S(2)}) collective-permute-start(bf16[4352,128]{1,0:T(8,128)(2,1)S(1)} %get-tuple-element.19), channel_id=1, source_target_pairs={{0,24},{1,7},{2,26},{3,1},{4,28},{5,3},{6,30},{7,5},{8,0},{9,15},{... | collective-permute-start | bytes 3342344 | tf_op jit(solution)/shard_map/ppermute | solution.py:233
  48.1 11.1 %collective-permute-start.12 = (bf16[1024,128]{1,0:T(8,128)(2,1)S(1)}, bf16[1024,128]{1,0:T(8,128)(2,1)S(1)}, u32[]{:S(2)}, u32[]{:S(2)}) collective-permute-start(bf16[1024,128]{1,0:T(8,128)(2,1)S(1)} %pad_maximum_fusion), channel_id=1, source_target_pairs={{0,2},{1,9},{2,4},{3,11},{4,6},{5,13},{6,0},{7,15},{8,10},{9,17},{... | collective-permute-start | bytes 786440 | tf_op jit(solution)/shard_map/ppermute | solution.py:233
  48.2 13.6 %collective-permute-start.13 = (bf16[1024,128]{1,0:T(8,128)(2,1)S(1)}, bf16[1024,128]{1,0:T(8,128)(2,1)S(1)}, u32[]{:S(2)}, u32[]{:S(2)}) collective-permute-start(bf16[1024,128]{1,0:T(8,128)(2,1)S(1)} %pad_maximum_fusion), channel_id=1, source_target_pairs={{0,4},{1,17},{2,6},{3,19},{4,0},{5,21},{6,2},{7,23},{8,12},{9,25},... | collective-permute-start | bytes 786440 | tf_op jit(solution)/shard_map/ppermute | solution.py:233
  59.2 7.9 %collective-permute-start.14 = (bf16[1024,128]{1,0:T(8,128)(2,1)S(1)}, bf16[1024,128]{1,0:T(8,128)(2,1)S(1)}, u32[]{:S(2)}, u32[]{:S(2)}) collective-permute-start(bf16[1024,128]{1,0:T(8,128)(2,1)S(1)} %pad_maximum_fusion), channel_id=1, source_target_pairs={{0,6},{1,25},{2,0},{3,27},{4,2},{5,29},{6,4},{7,31},{8,14},{9,1},{... | collective-permute-start | bytes 786440 | tf_op jit(solution)/shard_map/ppermute | solution.py:233
  67.8 34.0 %collective-permute-start.15 = (bf16[4096,128]{1,0:T(8,128)(2,1)}, bf16[4096,128]{1,0:T(8,128)(2,1)S(1)}, u32[]{:S(2)}, u32[]{:S(2)}) collective-permute-start(bf16[4096,128]{1,0:T(8,128)(2,1)} %constant_dynamic-update-slice_fusion.rest_0_), channel_id=1, source_target_pairs={{0,8},{1,3},{2,10},{3,5},{4,12},{5,7},{6,14},{7,1},{8,16},{9,11},{... | collective-permute-start | bytes 3145736 | tf_op jit(solution)/shard_map/ppermute | solution.py:233
  67.8 34.2 %collective-permute-start.16 = (bf16[4096,128]{1,0:T(8,128)(2,1)}, bf16[4096,128]{1,0:T(8,128)(2,1)}, u32[]{:S(2)}, u32[]{:S(2)}) collective-permute-start(bf16[4096,128]{1,0:T(8,128)(2,1)} %constant_dynamic-update-slice_fusion.rest_0_), channel_id=1, source_target_pairs={{0,24},{1,7},{2,26},{3,1},{4,28},{5,3},{6,30},{7,5},{8,0},{9,15},{... | collective-permute-start | bytes 3145736 | tf_op jit(solution)/shard_map/ppermute | solution.py:233
  75.8 14.9 %copy-start.6 = (s32[1,8,3]{1,0,2:T(1,128)S(1)}, s32[1,8,3]{1,0,2:T(1,128)}, u32[]{:S(2)}) copy-start(s32[1,8,3]{1,0,2:T(1,128)} %param.11) | copy-start | bytes 292
  75.8 10.0 %collective-permute-start.7 = (bf16[1088,128]{1,0:T(8,128)(2,1)S(1)}, bf16[1088,128]{1,0:T(8,128)(2,1)S(1)}, u32[]{:S(2)}, u32[]{:S(2)}) collective-permute-start(bf16[1088,128]{1,0:T(8,128)(2,1)S(1)} %get-tuple-element.21), channel_id=1, source_target_pairs={{0,2},{1,9},{2,4},{3,11},{4,6},{5,13},{6,0},{7,15},{8,10},{9,17},{... | collective-permute-start | bytes 835592 | tf_op jit(solution)/shard_map/ppermute | solution.py:233
  75.9 13.5 %collective-permute-start.8 = (bf16[1088,128]{1,0:T(8,128)(2,1)S(1)}, bf16[1088,128]{1,0:T(8,128)(2,1)S(1)}, u32[]{:S(2)}, u32[]{:S(2)}) collective-permute-start(bf16[1088,128]{1,0:T(8,128)(2,1)S(1)} %get-tuple-element.22), channel_id=1, source_target_pairs={{0,4},{1,17},{2,6},{3,19},{4,0},{5,21},{6,2},{7,23},{8,12},{9,25},... | collective-permute-start | bytes 835592 | tf_op jit(solution)/shard_map/ppermute | solution.py:233
  78.7 10.7 %collective-permute-start.9 = (bf16[1088,128]{1,0:T(8,128)(2,1)S(1)}, bf16[1088,128]{1,0:T(8,128)(2,1)S(1)}, u32[]{:S(2)}, u32[]{:S(2)}) collective-permute-start(bf16[1088,128]{1,0:T(8,128)(2,1)S(1)} %get-tuple-element.23), channel_id=1, source_target_pairs={{0,6},{1,25},{2,0},{3,27},{4,2},{5,29},{6,4},{7,31},{8,14},{9,1},{... | collective-permute-start | bytes 835592 | tf_op jit(solution)/shard_map/ppermute | solution.py:233
  90.5 1.6 %collective-permute-start.10 = (f32[4,128,128]{2,1,0:T(8,128)S(1)}, f32[4,128,128]{2,1,0:T(8,128)S(1)}, u32[]{:S(2)}, u32[]{:S(2)}) collective-permute-start(f32[4,128,128]{2,1,0:T(8,128)S(1)} %get-tuple-element.25), channel_id=1, source_target_pairs={{0,1},{1,0},{2,3},{3,2},{4,5},{5,4},{6,7},{7,6},{8,9},{9,8},{10,11... | collective-permute-start | bytes 786440 | tf_op jit(solution)/shard_map/ppermute | solution.py:233
  94.0 45.5 %all-to-all-start = ((bf16[8,400,128]{2,1,0:T(8,128)(2,1)}), bf16[8,400,128]{2,1,0:T(8,128)(2,1)S(1)}, u32[]{:S(2)}, u32[]{:S(2)}) async-start(bf16[8,400,128]{2,1,0:T(8,128)(2,1)} %get-tuple-element.26), calls=%async_computation | async-start | bytes 1638400 | tf_op jit(solution)/shard_map/all_to_all | solution.py:329
  101.4 11.7 %collective-permute-start.19 = (bf16[4096,128]{1,0:T(8,128)(2,1)}, bf16[4096,128]{1,0:T(8,128)(2,1)S(1)}, u32[]{:S(2)}, u32[]{:S(2)}) collective-permute-start(bf16[4096,128]{1,0:T(8,128)(2,1)} %constant_dynamic-update-slice_fusion.rest_0_), channel_id=1, source_target_pairs={{0,1},{1,0},{2,3},{3,2},{4,5},{5,4},{6,7},{7,6},{8,9},{9,8},{10,11... | collective-permute-start | bytes 3145736 | tf_op jit(solution)/shard_map/ppermute | solution.py:233
  101.9 9.6 %collective-permute-start.17 = (bf16[2048,128]{1,0:T(8,128)(2,1)S(1)}, bf16[2048,128]{1,0:T(8,128)(2,1)S(1)}, u32[]{:S(2)}, u32[]{:S(2)}) collective-permute-start(bf16[2048,128]{1,0:T(8,128)(2,1)S(1)} %slice.8), channel_id=1, source_target_pairs={{0,8},{1,3},{2,10},{3,5},{4,12},{5,7},{6,14},{7,1},{8,16},{9,11},{... | collective-permute-start | bytes 1572872 | tf_op jit(solution)/shard_map/ppermute | solution.py:233
  103.1 9.4 %collective-permute-start.18 = (bf16[2048,128]{1,0:T(8,128)(2,1)S(1)}, bf16[2048,128]{1,0:T(8,128)(2,1)S(1)}, u32[]{:S(2)}, u32[]{:S(2)}) collective-permute-start(bf16[2048,128]{1,0:T(8,128)(2,1)S(1)} %slice.9), channel_id=1, source_target_pairs={{0,24},{1,7},{2,26},{3,1},{4,28},{5,3},{6,30},{7,5},{8,0},{9,15},{... | collective-permute-start | bytes 1572872 | tf_op jit(solution)/shard_map/ppermute | solution.py:233
  105.8 8.9 %collective-permute-start.20 = (bf16[4096,128]{1,0:T(8,128)(2,1)S(1)}, bf16[4096,128]{1,0:T(8,128)(2,1)S(1)}, u32[]{:S(2)}, u32[]{:S(2)}) collective-permute-start(bf16[4096,128]{1,0:T(8,128)(2,1)S(1)} %collective-permute-done.15.rest_1_), channel_id=1, source_target_pairs={{0,1},{1,0},{2,3},{3,2},{4,5},{5,4},{6,7},{7,6},{8,9},{9,8},{10,11... | collective-permute-start | bytes 3145736 | tf_op jit(solution)/shard_map/ppermute | solution.py:233
  106.4 8.3 %collective-permute-start.21 = (bf16[4096,128]{1,0:T(8,128)(2,1)}, bf16[4096,128]{1,0:T(8,128)(2,1)S(1)}, u32[]{:S(2)}, u32[]{:S(2)}) collective-permute-start(bf16[4096,128]{1,0:T(8,128)(2,1)} %collective-permute-done.16.rest_2_), channel_id=1, source_target_pairs={{0,1},{1,0},{2,3},{3,2},{4,5},{5,4},{6,7},{7,6},{8,9},{9,8},{10,11... | collective-permute-start | bytes 3145736 | tf_op jit(solution)/shard_map/ppermute | solution.py:233
  111.5 2.5 %collective-permute-start.22 = (bf16[2048,128]{1,0:T(8,128)(2,1)S(1)}, bf16[2048,128]{1,0:T(8,128)(2,1)S(1)}, u32[]{:S(2)}, u32[]{:S(2)}) collective-permute-start(bf16[2048,128]{1,0:T(8,128)(2,1)S(1)} %collective-permute-done.17.rest_3_), channel_id=1, source_target_pairs={{0,1},{1,0},{2,3},{3,2},{4,5},{5,4},{6,7},{7,6},{8,9},{9,8},{10,11... | collective-permute-start | bytes 1572872 | tf_op jit(solution)/shard_map/ppermute | solution.py:233
  112.4 2.3 %collective-permute-start.23 = (bf16[2048,128]{1,0:T(8,128)(2,1)S(1)}, bf16[2048,128]{1,0:T(8,128)(2,1)S(1)}, u32[]{:S(2)}, u32[]{:S(2)}) collective-permute-start(bf16[2048,128]{1,0:T(8,128)(2,1)S(1)} %collective-permute-done.18.rest_4_), channel_id=1, source_target_pairs={{0,1},{1,0},{2,3},{3,2},{4,5},{5,4},{6,7},{7,6},{8,9},{9,8},{10,11... | collective-permute-start | bytes 1572872 | tf_op jit(solution)/shard_map/ppermute | solution.py:233
  114.7 3.1 %copy-start.2 = (bf16[256,14336]{1,0:T(8,128)(2,1)S(1)}, bf16[256,14336]{1,0:T(8,128)(2,1)}, u32[]{:S(2)}) copy-start(bf16[256,14336]{1,0:T(8,128)(2,1)} %grad.13) | copy-start | bytes 22020100
